TPU v7x, 32 devices: a whole 2x2x4 slice. The times are simulated.
32 devices in a mesh: groups: 2 (over y), ctx: 8 (over z, x), head: 2 (over core).
Axes of the slice: x: 2, y: 2, z: 4, core: 2. Of those that a mesh axis runs over, the one named last changes fastest.
Arguments:
- tokens: bfloat16 [6144, 4096], P(('groups', 'ctx'), 'head'), parts along dimension 0, may hold values from -6 to 6
- w_query: bfloat16 [4096, 2048], P('ctx', 'head'), may hold values from -0.09375 to 0.09375
- w_key: bfloat16 [4096, 2048], P('ctx', 'head'), may hold values from -0.09375 to 0.09375
- w_value: bfloat16 [4096, 2048], P('ctx', 'head'), may hold values from -0.09375 to 0.09375
- w_out: bfloat16 [2048, 4096], P('head'), may hold values from -0.125 to 0.125
Outputs:
- layer_out: bfloat16 [6144, 4096], P(('groups', 'ctx'), 'head'), parts along dimension 0
There are 2 independent parts, one for each index of `groups`. A program takes and returns all parts, laid end to end along the dimension named above; an argument that names none is the same for every part. Nothing has to cross between parts.
All inputs are finite; a program needn't handle non-finite values.
Results may differ from a plain program's by a relative error of at most 0.0067.
Values may be sent and summed in bfloat16 or wider, within the bound.
No kernel may reach another device: no remote copies, remote signals or barrier semaphores. Data moves between devices by JAX's collectives and lax.ppermute only.
A program may use at most 128 MiB of HBM per device.

v0:
```python
import jax
import jax.numpy as jnp
from jax import lax
from jax.sharding import PartitionSpec as P

HDIM = 128


def carried_in(value, axis, join, neutral):
    count, mine = (lax.axis_size(axis), lax.axis_index(axis))
    pieces = lax.all_gather(value, axis)
    total = jnp.full_like(value, 0) + jnp.asarray(neutral, value.dtype)

    def lap(position, total):
        longer = join(total, pieces[position])
        return jnp.where(position < mine, longer, total)

    return lax.fori_loop(0, count - 1, lap, total)


def add_panel(gathered, panel):
    return jnp.dot(gathered, panel, preferred_element_type=jnp.float32)


def combine_sum(earlier_sum, later_sum):
    return earlier_sum + later_sum


def split_heads(matrix):
    return matrix.reshape(matrix.shape[0], matrix.shape[1] // HDIM, HDIM)


def prefix_states(key_rows, value_rows):
    own_state = jnp.einsum("thd,the->hde", key_rows, value_rows, preferred_element_type=jnp.float32)
    return carried_in(own_state, "ctx", combine_sum, jnp.zeros_like(own_state))


def local(tokens, w_query, w_key, w_value, w_out):
    gathered = lax.all_gather(tokens, "head", axis=1, tiled=True)
    row_count = gathered.shape[0]

    def add_one(panel):
        return add_panel(gathered, panel)

    query_sum = add_one(lax.all_gather(w_query, "ctx", axis=0, tiled=True))
    key_sum = add_one(lax.all_gather(w_key, "ctx", axis=0, tiled=True))
    value_sum = add_one(lax.all_gather(w_value, "ctx", axis=0, tiled=True))
    key_rows = split_heads(jax.nn.silu(key_sum).astype(jnp.bfloat16))
    value_rows = split_heads(value_sum.astype(jnp.bfloat16))
    earlier = prefix_states(key_rows, value_rows)
    query_rows = split_heads(jax.nn.silu(query_sum).astype(jnp.bfloat16))
    position = lax.broadcasted_iota(jnp.int32, (row_count, row_count), 0)
    other = lax.broadcasted_iota(jnp.int32, (row_count, row_count), 1)
    causal = other <= position
    scores = jnp.einsum("thd,shd->hts", query_rows, key_rows, preferred_element_type=jnp.float32)
    weights = jnp.where(causal[None], scores, 0.0).astype(jnp.bfloat16)
    mixed = jnp.einsum("hts,she->the", weights, value_rows, preferred_element_type=jnp.float32)
    mixed = mixed + jnp.einsum(
        "thd,hde->the", query_rows, earlier.astype(jnp.bfloat16), preferred_element_type=jnp.float32
    )
    normed = mixed * lax.rsqrt(jnp.mean(mixed * mixed, axis=-1, keepdims=True) + 1e-06)
    normed = normed.astype(jnp.bfloat16).reshape(row_count, -1)
    head_terms = jnp.dot(normed, w_out, preferred_element_type=jnp.float32)
    return lax.psum_scatter(head_terms, "head", scatter_dimension=1, tiled=True).astype(
        jnp.bfloat16
    )


def solution(mesh):
    in_specs = (
        P(("groups", "ctx"), "head"),
        P("ctx", "head"),
        P("ctx", "head"),
        P("ctx", "head"),
        P("head", None),
    )
    out_specs = P(("groups", "ctx"), "head")
    return jax.shard_map(local, mesh=mesh, in_specs=in_specs, out_specs=out_specs, check_vma=False)
```

profile of v0, /device:TPU:0, one launch (start us, length us, event | category | flops | bytes accessed | tf_op | source)
XLA Modules:
  0.0 518.0 jit_solution(9432414339889200614)
XLA Ops:
  6.5 0.0 all-gather.7.cloned.1.call-start
  6.5 0.7 all-gather.7.cloned.1.call-update
  7.3 0.0 all-gather.13.cloned.1.call-start
  7.3 0.7 all-gather.13.cloned.1.call-update
  8.0 0.0 all-gather.9.cloned.1.call-start
  8.1 0.7 all-gather.9.cloned.1.call-update
  8.7 0.0 all-gather.11.cloned.1.call-start
  8.8 0.5 all-gather.11.cloned.1.call-update
  9.3 0.0 all-gather.15.cloned.1.call-start
  9.4 14.4 %all-gather.7.cloned.1.call-done = bf16[384,4096]{1,0:T(8,128)(2,1)} async-done(((bf16[384,2048]{1,0:T(8,128)(2,1)}), bf16[384,4096]{1,0:T(8,128)(2,1)}) %all-gather.7.cloned.1.call-update) | async-done | bytes 3145744 | tf_op jit(solution)/shard_map/all_gather | solution.py:39
  23.8 128.2 %all-gather.13.cloned.1.call-done = bf16[4096,1024]{1,0:T(8,128)(2,1)} async-done(((bf16[512,1024]{1,0:T(8,128)(2,1)}), bf16[4096,1024]{1,0:T(8,128)(2,1)}) %all-gather.13.cloned.1.call-update) | async-done | bytes 8388624 | tf_op jit(solution)/shard_map/all_gather | solution.py:46
  152.0 7.9 %multiply_convert_fusion = bf16[384,1024]{1,0:T(8,128)(2,1)S(1)} fusion(bf16[384,4096]{1,0:T(8,128)(2,1)} %all-gather.7.cloned.1.call-done, bf16[4096,1024]{1,0:T(8,128)(2,1)} %all-gather.13.cloned.1.call-done), kind=kOutput, calls=%fused_computation.10 | convolution fusion | flops 3223191552 | bytes 12320768 | tf_op jit(solution)/shard_map/dot_general | solution.py:22
  159.9 0.4 copy.17
  160.3 116.9 %all-gather.9.cloned.1.call-done = bf16[4096,1024]{1,0:T(8,128)(2,1)} async-done(((bf16[512,1024]{1,0:T(8,128)(2,1)}), bf16[4096,1024]{1,0:T(8,128)(2,1)}) %all-gather.9.cloned.1.call-update) | async-done | bytes 8388624 | tf_op jit(solution)/shard_map/all_gather | solution.py:47
  277.2 7.7 %fusion.7 = bf16[48,8,8,128]{3,2,1,0:T(8,128)(2,1)S(1)} fusion(bf16[384,4096]{1,0:T(8,128)(2,1)} %all-gather.7.cloned.1.call-done, bf16[4096,1024]{1,0:T(8,128)(2,1)} %all-gather.9.cloned.1.call-done), kind=kOutput, calls=%fused_computation.14 | convolution fusion | flops 3221618688 | bytes 12320768 | tf_op jit(solution)/shard_map/dot_general | solution.py:22
  285.0 0.0 copy-start.1
  285.0 0.9 copy-done.1
  285.9 1.2 fusion.12
  287.1 0.0 all-gather.15.cloned.1.call-update
  287.1 0.2 reduce-scatter.2.cloned.1.call-start
  287.4 114.9 %all-gather.11.cloned.1.call-done = bf16[4096,1024]{1,0:T(8,128)(2,1)} async-done(((bf16[512,1024]{1,0:T(8,128)(2,1)}), bf16[4096,1024]{1,0:T(8,128)(2,1)}) %all-gather.11.cloned.1.call-update) | async-done | bytes 8388624 | tf_op jit(solution)/shard_map/all_gather | solution.py:45
  402.3 8.8 %fusion.14 = bf16[48,8,8,128]{3,2,1,0:T(8,128)(2,1)} fusion(bf16[384,4096]{1,0:T(8,128)(2,1)} %all-gather.7.cloned.1.call-done, bf16[4096,1024]{1,0:T(8,128)(2,1)} %all-gather.11.cloned.1.call-done), kind=kOutput, calls=%fused_computation.20 | convolution fusion | flops 3223191552 | bytes 12320768 | tf_op jit(solution)/shard_map/dot_general | solution.py:22
  411.1 2.9 fusion
  414.0 61.9 %all-gather.15.cloned.1.call-done = f32[64,128,128]{2,1,0:T(8,128)} async-done(((f32[8,128,128]{2,1,0:T(8,128)}), f32[64,128,128]{2,1,0:T(8,128)}) %all-gather.15.cloned.1.call-update) | async-done | bytes 4194320 | tf_op jit(solution)/shard_map/all_gather | solution.py:11
  475.9 0.0 copy-start
  475.9 8.8 %while.14 = (s32[]{:T(128)}, f32[8,128,128]{2,1,0:T(8,128)S(1)}, s32[]{:T(128)}, f32[8,8,128,128]{3,2,1,0:T(8,128)}, s32[]{:T(128)}, /*index=5*/s32[]{:T(128)}) while((s32[]{:T(128)}, f32[8,128,128]{2,1,0:T(8,128)S(1)}, s32[]{:T(128)}, f32[8,8,128,128]{3,2,1,0:T(8,128)}, s32[]{:T(128)}, /*index=5*/s32[]{:T(128)}) %tuple.48), condition=%wide.region_1.2_spmd.clone, body=%wide.region_0.1_spmd.clone.sunk | while | flops 393220 | bytes 1572957 | solution.py:18
  475.9 1.3 add_select_fusion.2
  477.2 1.2 add_select_fusion.2
  478.5 1.2 add_select_fusion.2
  479.7 1.2 add_select_fusion.2
  481.0 1.2 add_select_fusion.2
  482.2 1.2 add_select_fusion.2
  483.5 1.2 add_select_fusion.2
  484.7 0.0 copy-done
  484.7 0.5 fusion.5
  485.2 0.2 fusion.6
  485.4 9.5 %fusion.22 = f32[384,4096]{1,0:T(8,128)} fusion(bf16[384,1024]{0,1:T(8,128)(2,1)S(1)} %bitcast.43, bf16[1024,4096]{1,0:T(8,128)(2,1)} %param.11), kind=kOutput, calls=%fused_computation.29 | convolution fusion | flops 3221225472 | bytes 15466496 | tf_op jit(solution)/shard_map/dot_general | solution.py:63
  494.9 0.0 reduce-scatter.2.cloned.1.call-update
  495.0 12.9 %reduce-scatter.2.cloned.1.call-done = f32[384,2048]{1,0:T(8,128)} async-done(((f32[384,4096]{1,0:T(8,128)}), f32[384,2048]{1,0:T(8,128)}) %reduce-scatter.2.cloned.1.call-update) | async-done | bytes 3145744 | tf_op jit(solution)/shard_map/reduce_scatter | solution.py:64
  507.9 3.3 convert_element_type.27
  (3 shorter events, 0.1 us)
Async XLA Ops:
  6.5 17.2 %all-gather.7.cloned.1.call-start = ((), (), s32[]{:S(2)}) async-start(), calls=%async_computation.1 | async-start | bytes 4718592 | tf_op jit(solution)/shard_map/all_gather | solution.py:39
  7.3 144.8 %all-gather.13.cloned.1.call-start = ((), (), s32[]{:S(2)}) async-start(), calls=%async_computation.4 | async-start | bytes 9437184 | tf_op jit(solution)/shard_map/all_gather | solution.py:46
  8.0 269.2 %all-gather.9.cloned.1.call-start = ((), (), s32[]{:S(2)}) async-start(), calls=%async_computation.2 | async-start | bytes 9437184 | tf_op jit(solution)/shard_map/all_gather | solution.py:47
  8.7 393.6 %all-gather.11.cloned.1.call-start = ((), (), s32[]{:S(2)}) async-start(), calls=%async_computation.3 | async-start | bytes 9437184 | tf_op jit(solution)/shard_map/all_gather | solution.py:45
  9.3 466.6 %all-gather.15.cloned.1.call-start = ((), (), s32[]{:S(2)}) async-start(), calls=%async_computation.6 | async-start | bytes 4718592 | tf_op jit(solution)/shard_map/all_gather | solution.py:11
  285.0 0.9 copy-start.1
  287.1 220.8 %reduce-scatter.2.cloned.1.call-start = ((), (), s32[]{:S(2)}) async-start(), calls=%async_computation.5 | async-start | bytes 9437184 | tf_op jit(solution)/shard_map/reduce_scatter | solution.py:64
  475.9 8.8 %copy-start = (bf16[48,8,8,128]{3,2,1,0:T(8,128)(2,1)S(1)}, bf16[48,8,8,128]{3,2,1,0:T(8,128)(2,1)}, u32[]{:S(2)}) copy-start(bf16[48,8,8,128]{3,2,1,0:T(8,128)(2,1)} %fusion.14) | copy-start | bytes 2359300
Sparse Core Ops, SparseCore 0:
  8.9 14.8 all-gather.6
  25.9 126.0 all-gather.12
  154.1 123.0 all-gather.8
  279.2 123.0 all-gather.10
  404.3 71.5 all-gather.14
  495.1 12.7 reduce-scatter.1
where the time goes:
time: 519 us; the launch traced here: 518 us
  waiting for transfers between devices  452 us (87%)
  matrix products  38.5 us (7%)
  between operations  13.6 us (3%)
  other arithmetic  12.1 us (2%)
    all_gather x1, waiting for transfers between devices, local(): key_sum = add_one(lax.all_gather(w_key, 'ctx', axis=0, tiled=True))  128 us
    all_gather x1, waiting for transfers between devices, local(): value_sum = add_one(lax.all_gather(w_value, 'ctx', axis=0, tiled=True))  117 us
    all_gather x1, waiting for transfers between devices, local(): query_sum = add_one(lax.all_gather(w_query, 'ctx', axis=0, tiled=True))  115 us
    all_gather x1, waiting for transfers between devices, carried_in(): pieces = lax.all_gather(value, axis)  61.9 us
    dot_general x3, matrix products, add_panel(): return jnp.dot(gathered, panel, preferred_element_type=jnp.float32)  24.4 us
    all_gather x1, waiting for transfers between devices, local(): gathered = lax.all_gather(tokens, 'head', axis=1, tiled=True)  14.4 us
    reduce_scatter x1, waiting for transfers between devices, local(): lax.psum_scatter(head_terms, 'head', scatter_dimension=1, tiled=True)  12.9 us
  transfers between devices with their start and end apart: 6, of which 6 were waited for; matrix products, arithmetic and copies ran while one was open for 6% of the time, Pallas kernels for 0%

commit v1 on v0

--- a/solution.py
+++ b/solution.py
@@ -1,9 +1,38 @@
+import functools
 import jax
 import jax.numpy as jnp
 from jax import lax
 from jax.sharding import PartitionSpec as P
 
 HDIM = 128
+
+
+def balance_flows(my_data, mesh_dim, k_dim):
+    local_next = lax.axis_size(mesh_dim)
+    last = lax.axis_index(mesh_dim)
+    step_out, far_arr, tall = (local_next, last, my_data.shape[k_dim])
+    by_place = [(nth, (nth + 1) % step_out) for nth in range(step_out)]
+    so_far_all = [(nth, (nth - 1) % step_out) for nth in range(step_out)]
+    vec_out = jnp.zeros(
+        (*my_data.shape[:k_dim], step_out * tall, *my_data.shape[k_dim + 1 :]), my_data.dtype
+    )
+    vec_out = lax.dynamic_update_slice_in_dim(vec_out, my_data, far_arr * tall, axis=k_dim)
+    seen_now = mid_arr = my_data
+    extra = step_out // 2
+    for num in range(1, extra + 1):
+        seen_now = lax.ppermute(seen_now, mesh_dim, by_place)
+        vec_out = lax.dynamic_update_slice_in_dim(
+            vec_out, seen_now, (far_arr - num) % step_out * tall, axis=k_dim
+        )
+        if num < step_out - extra:
+            mid_arr = lax.ppermute(mid_arr, mesh_dim, so_far_all)
+            vec_out = lax.dynamic_update_slice_in_dim(
+                vec_out, mid_arr, (far_arr + num) % step_out * tall, axis=k_dim
+            )
+    return vec_out
+
+
+track_the_squares = functools.partial(balance_flows, mesh_dim="ctx", k_dim=0)
 
 
 def carried_in(value, axis, join, neutral):
@@ -43,7 +72,7 @@
         return add_panel(gathered, panel)
 
     query_sum = add_one(lax.all_gather(w_query, "ctx", axis=0, tiled=True))
-    key_sum = add_one(lax.all_gather(w_key, "ctx", axis=0, tiled=True))
+    key_sum = add_one(track_the_squares(w_key))
     value_sum = add_one(lax.all_gather(w_value, "ctx", axis=0, tiled=True))
     key_rows = split_heads(jax.nn.silu(key_sum).astype(jnp.bfloat16))
     value_rows = split_heads(value_sum.astype(jnp.bfloat16))

time: 519 us -> 491 us (0.946)
  waiting for transfers between devices: 452 us -> 364 us
  starting transfers between devices: 0.38 us -> 43.1 us
  local copies, waits for them, and re-layouts: 1.3 us -> 18.1 us
    ppermute x0 -> x7, waiting for transfers between devices: none -> 178 us  [the longest x4 178 us: balance_flows(): seen_now = lax.ppermute(seen_now, mesh_dim, by_place)]
    all_gather x1 -> x0, waiting for transfers between devices: 128 us -> none  [local(): key_sum = add_one(lax.all_gather(w_key, 'ctx', axis=0, tiled=True))]
    all_gather x1, waiting for transfers between devices: 117 us -> 0.02 us  [local(): value_sum = add_one(lax.all_gather(w_value, 'ctx', axis=0, tiled=True))]
    ppermute x0 -> x7, starting transfers between devices: none -> 42.7 us  [the longest x3 32.3 us: balance_flows(): mid_arr = lax.ppermute(mid_arr, mesh_dim, so_far_all)]
    all_gather x1, waiting for transfers between devices: 14.4 us -> 0.01 us  [local(): gathered = lax.all_gather(tokens, 'head', axis=1, tiled=True)]
    dynamic_update_slice x0 -> x8, local copies, waits for them, and re-layouts: none -> 13.3 us  [the longest x4 6.72 us: balance_flows(): lax.dynamic_update_slice_in_dim(vec_out, seen_now, (far_arr - num) % step...]
    all_gather x1, waiting for transfers between devices: 115 us -> 109 us  [local(): query_sum = add_one(lax.all_gather(w_query, 'ctx', axis=0, tiled=True))]
  transfers between devices with their start and end apart: 6 -> 12, of which waited for: 6 -> 7; matrix products, arithmetic and copies ran while one was open for 6% -> 10% of each run, Pallas kernels for 0% -> 0%
where the time goes in v1:
time: 491 us; the launch traced here: 490 us
  waiting for transfers between devices  364 us (74%)
  starting transfers between devices  43.1 us (9%)
  matrix products  39.6 us (8%)
  local copies, waits for them, and re-layouts  18.1 us (4%)
  between operations  13.3 us (3%)
  other arithmetic  12.1 us (2%)
    ppermute x4, waiting for transfers between devices, balance_flows(): seen_now = lax.ppermute(seen_now, mesh_dim, by_place)  178 us
    all_gather x1, waiting for transfers between devices, local(): query_sum = add_one(lax.all_gather(w_query, 'ctx', axis=0, tiled=True))  109 us
    all_gather x1, waiting for transfers between devices, carried_in(): pieces = lax.all_gather(value, axis)  61.9 us
    ppermute x3, starting transfers between devices, balance_flows(): mid_arr = lax.ppermute(mid_arr, mesh_dim, so_far_all)  32.3 us
    dot_general x3, matrix products, add_panel(): return jnp.dot(gathered, panel, preferred_element_type=jnp.float32)  25.5 us
    reduce_scatter x1, waiting for transfers between devices, local(): lax.psum_scatter(head_terms, 'head', scatter_dimension=1, tiled=True)  12.9 us
    ppermute x4, starting transfers between devices, balance_flows(): seen_now = lax.ppermute(seen_now, mesh_dim, by_place)  10.4 us
  transfers between devices with their start and end apart: 12, of which 7 were waited for; matrix products, arithmetic and copies ran while one was open for 10% of the time, Pallas kernels for 0%

profile of v1, /device:TPU:0, one launch (start us, length us, event | category | flops | bytes accessed | tf_op | source)
XLA Modules:
  0.0 490.1 jit_solution(11367794651571865066)
XLA Ops:
  6.5 0.7 all-gather.6.cloned.1.call-update
  7.3 0.0 all-gather.8.cloned.1.call-start
  7.3 0.7 all-gather.8.cloned.1.call-update
  8.0 0.0 all-gather.10.cloned.1.call-start
  8.1 0.7 all-gather.10.cloned.1.call-update
  8.8 0.0 all-gather.12.cloned.1.call-start
  8.8 3.0 collective-permute-start
  11.8 3.1 collective-permute-start.1
  14.9 53.3 %collective-permute-done = bf16[512,1024]{1,0:T(8,128)(2,1)S(1)} collective-permute-done((bf16[512,1024]{1,0:T(8,128)(2,1)}, bf16[512,1024]{1,0:T(8,128)(2,1)S(1)}, u32[]{:S(2)}, u32[]{:S(2)}) %collective-permute-start) | collective-permute-done | bytes 1048608 | tf_op jit(solution)/shard_map/ppermute | solution.py:23
  68.2 2.4 collective-permute-start.2
  70.6 3.0 collective-permute-start.3
  73.6 59.5 %collective-permute-done.2 = bf16[512,1024]{1,0:T(8,128)(2,1)S(1)} collective-permute-done((bf16[512,1024]{1,0:T(8,128)(2,1)S(1)}, bf16[512,1024]{1,0:T(8,128)(2,1)S(1)}, u32[]{:S(2)}, u32[]{:S(2)}) %collective-permute-start.2) | collective-permute-done | bytes 1048608 | tf_op jit(solution)/shard_map/ppermute | solution.py:23
  133.1 2.5 collective-permute-start.4
  135.6 26.1 %collective-permute-start.5 = (bf16[512,1024]{1,0:T(8,128)(2,1)}, bf16[512,1024]{1,0:T(8,128)(2,1)}, u32[]{:S(2)}, u32[]{:S(2)}) collective-permute-start(bf16[512,1024]{1,0:T(8,128)(2,1)} %collective-permute-done.3), channel_id=1, source_target_pairs={{0,14},{2,0},{4,2},{6,4},{8,6},{10,8},{12,10},{14,12},{1,15},{3,1}... | collective-permute-start | bytes 3145736 | tf_op jit(solution)/shard_map/ppermute | solution.py:28
  161.8 40.2 %collective-permute-done.4 = bf16[512,1024]{1,0:T(8,128)(2,1)} collective-permute-done((bf16[512,1024]{1,0:T(8,128)(2,1)S(1)}, bf16[512,1024]{1,0:T(8,128)(2,1)}, u32[]{:S(2)}, u32[]{:S(2)}) %collective-permute-start.4) | collective-permute-done | bytes 1048608 | tf_op jit(solution)/shard_map/ppermute | solution.py:23
  201.9 2.6 collective-permute-start.6
  204.5 4.3 broadcast_in_dim.21
  208.9 1.1 constant_dynamic-update-slice_fusion.7
  209.9 1.1 constant_dynamic-update-slice_fusion.6
  211.0 1.0 constant_dynamic-update-slice_fusion.5
  212.1 1.0 constant_dynamic-update-slice_fusion.4
  213.1 2.3 constant_dynamic-update-slice_fusion.3
  215.4 2.3 constant_dynamic-update-slice_fusion.2
  217.7 2.3 constant_dynamic-update-slice_fusion.1
  219.9 24.8 %collective-permute-done.6 = bf16[512,1024]{1,0:T(8,128)(2,1)} collective-permute-done((bf16[512,1024]{1,0:T(8,128)(2,1)}, bf16[512,1024]{1,0:T(8,128)(2,1)}, u32[]{:S(2)}, u32[]{:S(2)}) %collective-permute-start.6) | collective-permute-done | bytes 1048608 | tf_op jit(solution)/shard_map/ppermute | solution.py:23
  244.8 2.3 constant_dynamic-update-slice_fusion
  247.1 7.9 %fusion.10 = bf16[384,1024]{1,0:T(8,128)(2,1)S(1)} fusion(bf16[384,4096]{1,0:T(8,128)(2,1)} %all-gather.6.cloned.1.call-done, bf16[4096,1024]{1,0:T(8,128)(2,1)} %constant_dynamic-update-slice_fusion), kind=kOutput, calls=%fused_computation.16 | convolution fusion | flops 3223191552 | bytes 12320768 | tf_op jit(solution)/shard_map/dot_general | solution.py:51
  255.0 0.4 copy.20
  255.4 8.8 %fusion.11 = bf16[48,8,8,128]{3,2,1,0:T(8,128)(2,1)S(1)} fusion(bf16[384,4096]{1,0:T(8,128)(2,1)} %all-gather.6.cloned.1.call-done, bf16[4096,1024]{1,0:T(8,128)(2,1)} %all-gather.8.cloned.1.call-done), kind=kOutput, calls=%fused_computation.19 | convolution fusion | flops 3221618688 | bytes 12320768 | tf_op jit(solution)/shard_map/dot_general | solution.py:51
  264.2 1.2 fusion.16
  265.4 0.2 reduce-scatter.2.cloned.1.call-start
  265.6 109.2 %all-gather.10.cloned.1.call-done = bf16[4096,1024]{1,0:T(8,128)(2,1)} async-done(((bf16[512,1024]{1,0:T(8,128)(2,1)}), bf16[4096,1024]{1,0:T(8,128)(2,1)}) %all-gather.10.cloned.1.call-update) | async-done | bytes 8388624 | tf_op jit(solution)/shard_map/all_gather | solution.py:74
  374.9 8.8 %fusion.18 = bf16[48,8,8,128]{3,2,1,0:T(8,128)(2,1)} fusion(bf16[384,4096]{1,0:T(8,128)(2,1)} %all-gather.6.cloned.1.call-done, bf16[4096,1024]{1,0:T(8,128)(2,1)} %all-gather.10.cloned.1.call-done), kind=kOutput, calls=%fused_computation.25 | convolution fusion | flops 3223191552 | bytes 12320768 | tf_op jit(solution)/shard_map/dot_general | solution.py:51
  383.6 2.9 fusion
  386.6 61.9 %all-gather.12.cloned.1.call-done = f32[64,128,128]{2,1,0:T(8,128)} async-done(((f32[8,128,128]{2,1,0:T(8,128)}), f32[64,128,128]{2,1,0:T(8,128)}) %all-gather.12.cloned.1.call-update) | async-done | bytes 4194320 | tf_op jit(solution)/shard_map/all_gather | solution.py:40
  448.4 8.7 %while.14 = (s32[]{:T(128)}, f32[8,128,128]{2,1,0:T(8,128)S(1)}, s32[]{:T(128)}, f32[8,8,128,128]{3,2,1,0:T(8,128)}, s32[]{:T(128)}, /*index=5*/s32[]{:T(128)}) while((s32[]{:T(128)}, f32[8,128,128]{2,1,0:T(8,128)S(1)}, s32[]{:T(128)}, f32[8,8,128,128]{3,2,1,0:T(8,128)}, s32[]{:T(128)}, /*index=5*/s32[]{:T(128)}) %tuple.46), condition=%wide.region_1.2_spmd.clone, body=%wide.region_0.1_spmd.clone.sunk | while | flops 393220 | bytes 1572957 | solution.py:47
  448.4 1.2 add_select_fusion.2
  449.7 1.2 add_select_fusion.2
  450.9 1.2 add_select_fusion.2
  452.2 1.2 add_select_fusion.2
  453.4 1.2 add_select_fusion.2
  454.7 1.2 add_select_fusion.2
  455.9 1.2 add_select_fusion.2
  457.2 0.5 fusion.5
  457.7 0.2 fusion.6
  457.9 9.5 %fusion.26 = f32[384,4096]{1,0:T(8,128)} fusion(bf16[384,1024]{0,1:T(8,128)(2,1)S(1)} %bitcast.56, bf16[1024,4096]{1,0:T(8,128)(2,1)} %param.11), kind=kOutput, calls=%fused_computation.42 | convolution fusion | flops 3221225472 | bytes 15466496 | tf_op jit(solution)/shard_map/dot_general | solution.py:92
  467.4 12.9 %reduce-scatter.2.cloned.1.call-done = f32[384,2048]{1,0:T(8,128)} async-done(((f32[384,4096]{1,0:T(8,128)}), f32[384,2048]{1,0:T(8,128)}) %reduce-scatter.2.cloned.1.call-update) | async-done | bytes 3145744 | tf_op jit(solution)/shard_map/reduce_scatter | solution.py:93
  480.3 3.3 convert_element_type.27
  (21 shorter events, 0.1 us)
Async XLA Ops:
  6.5 240.5 %all-gather.6.cloned.1.call-start = ((), (), s32[]{:S(2)}) async-start(), calls=%async_computation.1 | async-start | bytes 4718592 | tf_op jit(solution)/shard_map/all_gather | solution.py:68
  7.3 248.1 %all-gather.8.cloned.1.call-start = ((), (), s32[]{:S(2)}) async-start(), calls=%async_computation.2 | async-start | bytes 9437184 | tf_op jit(solution)/shard_map/all_gather | solution.py:76
  8.0 200.9 %copy-start = (bf16[512,1024]{1,0:T(8,128)(2,1)S(1)}, bf16[512,1024]{1,0:T(8,128)(2,1)}, u32[]{:S(2)}) copy-start(bf16[512,1024]{1,0:T(8,128)(2,1)} %param.9) | copy-start | bytes 3145732
  8.0 366.8 %all-gather.10.cloned.1.call-start = ((), (), s32[]{:S(2)}) async-start(), calls=%async_computation.3 | async-start | bytes 9437184 | tf_op jit(solution)/shard_map/all_gather | solution.py:74
  8.8 439.7 %all-gather.12.cloned.1.call-start = ((), (), s32[]{:S(2)}) async-start(), calls=%async_computation.5 | async-start | bytes 4718592 | tf_op jit(solution)/shard_map/all_gather | solution.py:40
  8.8 59.4 %collective-permute-start = (bf16[512,1024]{1,0:T(8,128)(2,1)}, bf16[512,1024]{1,0:T(8,128)(2,1)S(1)}, u32[]{:S(2)}, u32[]{:S(2)}) collective-permute-start(bf16[512,1024]{1,0:T(8,128)(2,1)} %param.9), channel_id=1, source_target_pairs={{0,2},{2,4},{4,6},{6,8},{8,10},{10,12},{12,14},{14,0},{1,3},{3,5},... | collective-permute-start | bytes 3145736 | tf_op jit(solution)/shard_map/ppermute | solution.py:23
  11.8 58.8 %collective-permute-start.1 = (bf16[512,1024]{1,0:T(8,128)(2,1)}, bf16[512,1024]{1,0:T(8,128)(2,1)S(1)}, u32[]{:S(2)}, u32[]{:S(2)}) collective-permute-start(bf16[512,1024]{1,0:T(8,128)(2,1)} %param.9), channel_id=1, source_target_pairs={{0,14},{2,0},{4,2},{6,4},{8,6},{10,8},{12,10},{14,12},{1,15},{3,1}... | collective-permute-start | bytes 3145736 | tf_op jit(solution)/shard_map/ppermute | solution.py:28
  68.2 64.9 %collective-permute-start.2 = (bf16[512,1024]{1,0:T(8,128)(2,1)S(1)}, bf16[512,1024]{1,0:T(8,128)(2,1)S(1)}, u32[]{:S(2)}, u32[]{:S(2)}) collective-permute-start(bf16[512,1024]{1,0:T(8,128)(2,1)S(1)} %collective-permute-done), channel_id=1, source_target_pairs={{0,2},{2,4},{4,6},{6,8},{8,10},{10,12},{12,14},{14,0},{1,3},{3,5},... | collective-permute-start | bytes 3145736 | tf_op jit(solution)/shard_map/ppermute | solution.py:23
  70.6 65.0 %collective-permute-start.3 = (bf16[512,1024]{1,0:T(8,128)(2,1)S(1)}, bf16[512,1024]{1,0:T(8,128)(2,1)}, u32[]{:S(2)}, u32[]{:S(2)}) collective-permute-start(bf16[512,1024]{1,0:T(8,128)(2,1)S(1)} %collective-permute-done.1), channel_id=1, source_target_pairs={{0,14},{2,0},{4,2},{6,4},{8,6},{10,8},{12,10},{14,12},{1,15},{3,1}... | collective-permute-start | bytes 3145736 | tf_op jit(solution)/shard_map/ppermute | solution.py:28
  133.1 2.5 copy-start.1
  133.1 68.8 %collective-permute-start.4 = (bf16[512,1024]{1,0:T(8,128)(2,1)S(1)}, bf16[512,1024]{1,0:T(8,128)(2,1)}, u32[]{:S(2)}, u32[]{:S(2)}) collective-permute-start(bf16[512,1024]{1,0:T(8,128)(2,1)S(1)} %collective-permute-done.2), channel_id=1, source_target_pairs={{0,2},{2,4},{4,6},{6,8},{8,10},{10,12},{12,14},{14,0},{1,3},{3,5},... | collective-permute-start | bytes 3145736 | tf_op jit(solution)/shard_map/ppermute | solution.py:23
  135.6 82.1 %collective-permute-start.5 = (bf16[512,1024]{1,0:T(8,128)(2,1)}, bf16[512,1024]{1,0:T(8,128)(2,1)}, u32[]{:S(2)}, u32[]{:S(2)}) collective-permute-start(bf16[512,1024]{1,0:T(8,128)(2,1)} %collective-permute-done.3), channel_id=1, source_target_pairs={{0,14},{2,0},{4,2},{6,4},{8,6},{10,8},{12,10},{14,12},{1,15},{3,1}... | collective-permute-start | bytes 3145736 | tf_op jit(solution)/shard_map/ppermute | solution.py:28
  201.9 42.8 %collective-permute-start.6 = (bf16[512,1024]{1,0:T(8,128)(2,1)}, bf16[512,1024]{1,0:T(8,128)(2,1)}, u32[]{:S(2)}, u32[]{:S(2)}) collective-permute-start(bf16[512,1024]{1,0:T(8,128)(2,1)} %collective-permute-done.4), channel_id=1, source_target_pairs={{0,2},{2,4},{4,6},{6,8},{8,10},{10,12},{12,14},{14,0},{1,3},{3,5},... | collective-permute-start | bytes 3145736 | tf_op jit(solution)/shard_map/ppermute | solution.py:23
  208.9 3.2 copy-start.2
  264.1 1.2 copy-start.4
  265.4 215.0 %reduce-scatter.2.cloned.1.call-start = ((), (), s32[]{:S(2)}) async-start(), calls=%async_computation.4 | async-start | bytes 9437184 | tf_op jit(solution)/shard_map/reduce_scatter | solution.py:93
  386.6 70.6 %copy-start.3 = (bf16[48,8,8,128]{3,2,1,0:T(8,128)(2,1)S(1)}, bf16[48,8,8,128]{3,2,1,0:T(8,128)(2,1)}, u32[]{:S(2)}) copy-start(bf16[48,8,8,128]{3,2,1,0:T(8,128)(2,1)} %fusion.18) | copy-start | bytes 2359300
Sparse Core Ops, SparseCore 0:
  8.9 14.8 all-gather.5
  25.9 223.9 all-gather.7
  252.0 122.8 all-gather.9
  376.8 71.5 all-gather.11
  467.5 12.7 reduce-scatter.1
